TPU v7x, 512 devices: a whole 4x4x16 slice. The times are simulated.
512 devices in a mesh: dp: 16 (over z), tensor: 32 (over x, y, core).
Axes of the slice: x: 4, y: 4, z: 16, core: 2. Of those that a mesh axis runs over, the one named last changes fastest.
Arguments:
- hidden: bfloat16 [14336, 4096], P('dp', 'tensor')
- gain: bfloat16 [4096], P('tensor'), may hold values from 0.5 to 1.5
- head_weight: bfloat16 [4096, 32000], P('dp', 'tensor')
- targets: int32 [14336], P('dp'), may hold values from 0 to 31999
- seq_ids: int32 [14336], P(('dp', 'tensor')), may hold values from 0 to 63, never falling along the last dimension, each value on 1 to 1792 neighbouring positions
- live: int32 [14336], P(('dp', 'tensor')), may hold values 0 or 1
Outputs:
- logprob: float32 [14336], P(('dp', 'tensor'))
- entropy: float32 [14336], P(('dp', 'tensor'))
- seq_mean: float32 [64], replicated
Inputs may be any that keep to these rules, and one draw needn't show every extreme that they name: `seq_ids`: sequence numbers never fall along the tokens; each sequence has 1 to 1792 tokens, one exactly 1792.
All inputs are finite; a program needn't handle non-finite values. No bound on the sum of `live` on one device may be relied on, other than what follows from the above.
Results may differ from a plain program's by a relative error of at most 0.0015.
Values may be sent and summed in bfloat16 or wider, within the bound.
No kernel may reach another device: no remote copies, remote signals or barrier semaphores. Data moves between devices by JAX's collectives and lax.ppermute only.
A program may use at most 64 MiB of HBM per device.

v0:
```python
import jax
import jax.numpy as jnp
from jax import lax
from jax.sharding import PartitionSpec as P

SEQ_DEV = 4


def body(hidden, gain, head_weight, targets, seq_ids, live):
    shards = lax.axis_size("tensor")
    rank = lax.axis_index("tensor")
    tok_rows = hidden.shape[0]
    share = tok_rows // shards
    vocab_dev = head_weight.shape[1]
    whole, gains = (
        lax.all_gather(hidden, "tensor", axis=1, tiled=True),
        lax.all_gather(gain, "tensor", axis=0, tiled=True),
    )
    values = whole.astype(jnp.float32)
    meansq = jnp.mean(values * values, axis=-1, keepdims=True)
    normed = (values * lax.rsqrt(meansq + 1e-05) * gains.astype(jnp.float32)).astype(jnp.bfloat16)
    scores = jnp.dot(
        normed,
        lax.all_gather(head_weight, "dp", axis=0, tiled=True),
        preferred_element_type=jnp.float32,
    )
    top = jnp.max(scores, axis=-1)
    shifted = scores - top[:, None]
    expo = jnp.exp(shifted)
    total = jnp.sum(expo, axis=-1)
    spread = jnp.sum(expo * shifted, axis=-1)
    local_ids = targets - rank * vocab_dev
    inside = (local_ids >= 0) & (local_ids < vocab_dev)
    picked = jnp.take_along_axis(scores, jnp.clip(local_ids, 0, vocab_dev - 1)[:, None], axis=1)[
        :, 0
    ]
    target_score = jnp.where(inside, picked, 0.0)
    offset = rank * share
    best = lax.pmax(top, "tensor")
    scale = jnp.exp(top - best)
    sums = lax.psum(
        (total * scale, (spread + (top - best) * total) * scale, target_score), "tensor"
    )
    g_top = lax.dynamic_slice_in_dim(best, offset, share, 0)
    g_total = lax.dynamic_slice_in_dim(sums[0], offset, share, 0)
    g_spread = lax.dynamic_slice_in_dim(sums[1], offset, share, 0)
    g_target = lax.dynamic_slice_in_dim(sums[2], offset, share, 0)
    weight = live.astype(jnp.float32)
    log_total = jnp.log(g_total)
    logprob = (g_target - g_top - log_total) * weight
    entropy = (log_total - g_spread / g_total) * weight
    seq_count = SEQ_DEV * lax.axis_size("dp")
    member = (seq_ids[:, None] == jnp.arange(seq_count)[None, :]).astype(jnp.float32)
    seq_sums = jnp.sum(member * logprob[:, None], axis=0)
    seq_live = jnp.sum(member * weight[:, None], axis=0)
    seq_sums, seq_live = lax.psum((seq_sums, seq_live), ("dp", "tensor"))
    seq_mean = seq_sums / jnp.maximum(seq_live, 1.0)
    return (logprob, entropy, seq_mean)


def solution(mesh):
    placed = (
        P("dp", "tensor"),
        P("tensor"),
        P("dp", "tensor"),
        P("dp"),
        P(("dp", "tensor")),
        P(("dp", "tensor")),
    )
    return jax.shard_map(
        body,
        mesh=mesh,
        in_specs=placed,
        out_specs=(P(("dp", "tensor")), P(("dp", "tensor")), P()),
        check_vma=False,
    )
```

profile of v0, /device:TPU:1, one launch (start us, length us, event | category | flops | bytes accessed | tf_op | source)
XLA Modules:
  0.0 559.9 jit_solution(8000703077066795527)
XLA Ops:
  7.2 0.0 all-gather.4.cloned.1.call-start
  7.2 0.7 all-gather.4.cloned.1.call-update
  7.9 0.0 all-gather.6.cloned.1.call-start
  7.9 0.7 all-gather.6.cloned.1.call-update
  8.7 24.1 %all-gather = bf16[32,1,128]{2,1,0:T(2,128)(2,1)S(1)} all-gather(bf16[1,1,128]{2,1,0:T(2,128)(2,1)} %bitcast.6), channel_id=1, replica_groups=mesh['dp'=16,'tensor'=32] {'tensor'}, dimensions={0}, use_global_device_ids=true | all-gather | bytes 8448 | tf_op jit(solution)/shard_map/all_gather | solution.py:17
  32.8 0.7 compare_select_fusion
  33.5 0.7 convert_element_type.16
  34.2 54.0 %all-gather.4.cloned.1.call-done = bf16[896,4096]{1,0:T(8,128)(2,1)} async-done(((bf16[896,128]{1,0:T(8,128)(2,1)}), bf16[896,4096]{1,0:T(8,128)(2,1)}) %all-gather.4.cloned.1.call-update) | async-done | bytes 7340048 | tf_op jit(solution)/shard_map/all_gather | solution.py:16
  88.3 4.6 fusion
  92.8 114.5 %all-gather.6.cloned.1.call-done = bf16[4096,1000]{0,1:T(8,128)(2,1)} async-done(((bf16[256,1000]{0,1:T(8,128)(2,1)}), bf16[4096,1000]{0,1:T(8,128)(2,1)}) %all-gather.6.cloned.1.call-update) | async-done | bytes 8192016 | tf_op jit(solution)/shard_map/all_gather | solution.py:24
  207.3 14.7 %fusion.12 = (f32[896]{0:T(1024)S(1)}, f32[896,1000]{0,1:T(8,128)}) fusion(bf16[4096,1000]{0,1:T(8,128)(2,1)} %all-gather.6.cloned.1.call-done, bf16[896,4096]{1,0:T(8,128)(2,1)} %all-gather.4.cloned.1.call-done, f32[4096]{0:T(1024)S(1)} %bitcast.5, f32[896]{0:T(1024)S(1)} %add_rsqrt_fusion), kind=kOutput, calls=%fused_computation.30 | convolution fusion | flops 7355607040 | bytes 19139584 | tf_op jit(solution)/shard_map/dot_general | solution.py:22
  222.1 0.0 copy-start
  222.1 0.0 copy-start.3
  222.1 0.0 copy-start.2
  222.1 73.2 %pmax.7 = f32[896]{0:T(1024)S(1)} all-reduce(f32[896]{0:T(1024)S(1)} %get-tuple-element.16), channel_id=1, replica_groups=mesh['dp'=16,'tensor'=32] {'tensor'}, use_global_device_ids=true, to_apply=%region_3.0 | all-reduce | flops 896 | bytes 7168 | tf_op jit(solution)/shard_map/pmax | solution.py:39
  295.2 2.7 fusion.7
  298.0 30.1 %gather_fusion = f32[896]{0:T(1024)S(1)} fusion(f32[896,1000]{0,1:T(8,128)} %get-tuple-element.17, s32[896]{0:T(1024)S(1)} %fusion.11), kind=kCustom, calls=%fused_computation | custom fusion | bytes 14336 | tf_op jit(solution)/shard_map/jit(take_along_axis)/gather | solution.py:34
  328.1 0.0 copy-done
  328.2 121.3 %all-reduce.1 = (f32[896]{0:T(1024)S(1)}, f32[896]{0:T(1024)S(1)}, f32[896]{0:T(1024)S(1)}) all-reduce(f32[896]{0:T(1024)S(1)} %select_select_fusion, f32[896]{0:T(1024)S(1)} %get-tuple-element.13, f32[896]{0:T(1024)S(1)} %get-tuple-element.12), channel_id=1, replica_groups=mesh['dp'=16,'tensor'=32] {'tensor'}, use_global_device_ids=true, to_apply=%region_1.0 | all-reduce | flops 2688 | bytes 21504 | tf_op jit(solution)/shard_map/psum | solution.py:41
  449.4 0.0 copy-done.3
  449.4 0.6 subtract_multiply_fusion
  450.0 0.0 copy-start.1
  450.0 0.0 copy-done.2
  450.0 0.1 select_reduce_fusion
  450.1 102.4 %all-reduce = (f32[64]{0:T(128)S(1)}, f32[64]{0:T(128)S(1)}) all-reduce(f32[64]{0:T(128)S(1)} %get-tuple-element.6, f32[64]{0:T(128)S(1)} %get-tuple-element.5), channel_id=1, replica_groups=mesh['dp'=16,'tensor'=32] {'dp','tensor'}, use_global_device_ids=true, to_apply=%region_9.10 | all-reduce | flops 128 | bytes 1024 | tf_op jit(solution)/shard_map/psum | solution.py:56
  552.5 0.5 maximum_divide_fusion
  553.1 0.0 copy-done.1
  (8 shorter events, 0.1 us)
Async XLA Ops:
  7.2 81.1 %all-gather.4.cloned.1.call-start = ((), (), s32[]{:S(2)}) async-start(), calls=%async_computation | async-start | bytes 7569408 | tf_op jit(solution)/shard_map/all_gather | solution.py:16
  7.9 199.4 %all-gather.6.cloned.1.call-start = ((), (), s32[]{:S(2)}) async-start(), calls=%async_computation.1 | async-start | bytes 8704000 | tf_op jit(solution)/shard_map/all_gather | solution.py:24
  222.1 106.1 %copy-start = (s32[896]{0:T(1024)S(1)}, s32[896]{0:T(1024)}, u32[]{:S(2)}) copy-start(s32[896]{0:T(1024)} %param.9) | copy-start | bytes 10756
  222.1 227.4 %copy-start.3 = (s32[28]{0:T(128)S(1)}, s32[28]{0:T(128)}, u32[]{:S(2)}) copy-start(s32[28]{0:T(128)} %param.11) | copy-start | bytes 340
  222.1 228.0 %copy-start.2 = (s32[28]{0:T(128)S(1)}, s32[28]{0:T(128)}, u32[]{:S(2)}) copy-start(s32[28]{0:T(128)} %param.10) | copy-start | bytes 340
  450.0 103.0 %copy-start.1 = (f32[28]{0:T(128)}, f32[28]{0:T(128)S(1)}, u32[]{:S(2)}) copy-start(f32[28]{0:T(128)S(1)} %get-tuple-element.15) | copy-start | bytes 340
Sparse Core Ops, SparseCore 0:
  11.0 77.1 all-gather.3
  90.3 117.0 all-gather.5
where the time goes:
time: 561 us; the launch traced here: 560 us
  blocking collectives  321 us (57%)
  waiting for transfers between devices  170 us (30%)
  local copies, waits for them, and re-layouts  30.2 us (5%)
  matrix products  14.7 us (3%)
  between operations  14.1 us (3%)
  other arithmetic  9.96 us (2%)
    psum x1, blocking collectives, body(): lax.psum((total * scale, (spread + (top - best) * total) * scale, target_...  121 us
    all_gather x1, waiting for transfers between devices, body(): lax.all_gather(head_weight, 'dp', axis=0, tiled=True)  114 us
    psum x1, blocking collectives, body(): seq_sums, seq_live = lax.psum((seq_sums, seq_live), ('dp', 'tensor'))  102 us
    pmax x1, blocking collectives, body(): best = lax.pmax(top, 'tensor')  73.2 us
    all_gather x1, waiting for transfers between devices, body(): lax.all_gather(hidden, 'tensor', axis=1, tiled=True)  54 us
    gather x1, local copies, waits for them, and re-layouts, body(): jnp.take_along_axis(scores, jnp.clip(local_ids, 0, vocab_dev - 1)[:, None...  30.1 us
    all_gather x1, blocking collectives, body(): lax.all_gather(gain, 'tensor', axis=0, tiled=True)  24.1 us
    dot_general x1, matrix products, body(): jnp.dot(normed, lax.all_gather(head_weight, 'dp', axis=0, tiled=True), pr...  14.7 us
  transfers between devices with their start and end apart: 2, of which 2 were waited for; matrix products, arithmetic and copies ran while one was open for 1% of the time, Pallas kernels for 0%

commit v1 on v0

--- a/solution.py
+++ b/solution.py
@@ -4,6 +4,11 @@
 from jax.sharding import PartitionSpec as P
 
 SEQ_DEV = 4
+
+
+def exchange_gather(value, mesh_axis, dim):
+    repeated = jnp.stack([value] * lax.axis_size(mesh_axis))
+    return jnp.concatenate(lax.all_to_all(repeated, mesh_axis, 0, 0), axis=dim)
 
 
 def body(hidden, gain, head_weight, targets, seq_ids, live):
@@ -13,7 +18,7 @@
     share = tok_rows // shards
     vocab_dev = head_weight.shape[1]
     whole, gains = (
-        lax.all_gather(hidden, "tensor", axis=1, tiled=True),
+        exchange_gather(hidden, "tensor", 1),
         lax.all_gather(gain, "tensor", axis=0, tiled=True),
     )
     values = whole.astype(jnp.float32)

time: 561 us -> 509 us (0.907)
  waiting for transfers between devices: 170 us -> 0.69 us
  blocking collectives: 321 us -> 415 us
  starting transfers between devices: 0.08 us -> 11.5 us
  other arithmetic: 9.96 us -> 16.6 us
    all_gather x1, waiting for transfers between devices: 114 us -> 0.01 us  [body(): lax.all_gather(head_weight, 'dp', axis=0, tiled=True)]
    all_gather x1, blocking collectives: 24.1 us -> 119 us  [body(): lax.all_gather(gain, 'tensor', axis=0, tiled=True)]
    all_gather x1 -> x0, waiting for transfers between devices: 54 us -> none  [body(): lax.all_gather(hidden, 'tensor', axis=1, tiled=True)]
    all_to_all x0 -> x1, starting transfers between devices: none -> 11.5 us  [exchange_gather(): return jnp.concatenate(lax.all_to_all(repeated, mesh_axis, 0, 0), axis=dim)]
    pmax x1, blocking collectives: 73.2 us -> 62.2 us  [body(): best = lax.pmax(top, 'tensor')]
    convert_element_type x0 -> x1, other arithmetic: none -> 7.82 us  [body(): (values * lax.rsqrt(meansq + 1e-05) * gains.astype(jnp.float32)).astype(j...]
  transfers between devices with their start and end apart: 2 -> 2, of which waited for: 2 -> 0; matrix products, arithmetic and copies ran while one was open for 1% -> 4% of each run, Pallas kernels for 0% -> 0%
where the time goes in v1:
time: 509 us; the launch traced here: 507 us
  blocking collectives  415 us (82%)
  local copies, waits for them, and re-layouts  35.3 us (7%)
  other arithmetic  16.6 us (3%)
  matrix products  14.5 us (3%)
  between operations  14.2 us (3%)
  starting transfers between devices  11.5 us (2%)
    psum x1, blocking collectives, body(): lax.psum((total * scale, (spread + (top - best) * total) * scale, target_...  126 us
    all_gather x1, blocking collectives, body(): lax.all_gather(gain, 'tensor', axis=0, tiled=True)  119 us
    psum x1, blocking collectives, body(): seq_sums, seq_live = lax.psum((seq_sums, seq_live), ('dp', 'tensor'))  107 us
    pmax x1, blocking collectives, body(): best = lax.pmax(top, 'tensor')  62.2 us
    gather x1, local copies, waits for them, and re-layouts, body(): jnp.take_along_axis(scores, jnp.clip(local_ids, 0, vocab_dev - 1)[:, None...  30.1 us
    dot_general x1, matrix products, body(): jnp.dot(normed, lax.all_gather(head_weight, 'dp', axis=0, tiled=True), pr...  14.5 us
    all_to_all x1, starting transfers between devices, exchange_gather(): return jnp.concatenate(lax.all_to_all(repeated, mesh_axis, 0, 0), axis=dim)  11.5 us
  transfers between devices with their start and end apart: 2, of which 0 were waited for; matrix products, arithmetic and copies ran while one was open for 4% of the time, Pallas kernels for 0%

profile of v1, /device:TPU:1, one launch (start us, length us, event | category | flops | bytes accessed | tf_op | source)
XLA Modules:
  0.0 507.4 jit_solution(12041670304629532942)
XLA Ops:
  7.2 0.0 all-gather.3.cloned.1.call-start
  7.2 0.7 all-gather.3.cloned.1.call-update
  7.9 1.1 copy.11
  9.0 4.1 stack.2
  13.0 0.0 copy-start.2
  13.1 0.0 copy-start
  13.1 0.0 copy-start.4
  13.1 11.5 %all-to-all-start = ((bf16[32,896,128]{1,2,0:T(8,128)(2,1)}), bf16[32,896,128]{1,2,0:T(8,128)(2,1)}, u32[]{:S(2)}, u32[]{:S(2)}) async-start(bf16[32,896,128]{1,2,0:T(8,128)(2,1)} %stack.2), calls=%async_computation | async-start | bytes 14680064 | tf_op jit(solution)/shard_map/all_to_all | solution.py:11
  24.6 0.0 copy-done.2
  24.6 119.4 %all-gather = bf16[32,1,128]{2,1,0:T(2,128)(2,1)S(1)} all-gather(bf16[1,1,128]{2,1,0:T(2,128)(2,1)S(1)} %bitcast.15), channel_id=1, replica_groups=mesh['dp'=16,'tensor'=32] {'tensor'}, dimensions={0}, use_global_device_ids=true | all-gather | bytes 8448 | tf_op jit(solution)/shard_map/all_gather | solution.py:22
  144.0 0.0 copy-done
  144.0 0.0 copy-done.4
  144.1 0.0 all-to-all-done
  144.1 4.8 multiply_reduce_fusion
  148.9 7.8 %fusion.1 = bf16[896,4096]{0,1:T(8,128)(2,1)} fusion(f32[4096]{0:T(1024)S(1)} %bitcast.14, f32[896]{0:T(1024)S(1)} %add_rsqrt_fusion, bf16[32,896,128]{1,2,0:T(8,128)(2,1)} %all-to-all-done), kind=kLoop, calls=%fused_computation.3 | loop fusion | flops 14680064 | bytes 14700032 | tf_op jit(solution)/shard_map/convert_element_type | solution.py:26
  156.7 0.0 all-gather.3.cloned.1.call-done
  156.7 14.5 %fusion.7 = (f32[896]{0:T(1024)S(1)}, f32[896,1000]{0,1:T(8,128)}) fusion(bf16[896,4096]{0,1:T(8,128)(2,1)} %fusion.1, bf16[4096,1000]{0,1:T(8,128)(2,1)} %all-gather.3.cloned.1.call-done), kind=kOutput, calls=%fused_computation.26 | convolution fusion | flops 7340926976 | bytes 19119616 | tf_op jit(solution)/shard_map/dot_general | solution.py:27
  171.2 0.0 copy-start.3
  171.2 62.2 %pmax.7 = f32[896]{0:T(1024)S(1)} all-reduce(f32[896]{0:T(1024)S(1)} %get-tuple-element.16), channel_id=1, replica_groups=mesh['dp'=16,'tensor'=32] {'tensor'}, use_global_device_ids=true, to_apply=%region_3.0 | all-reduce | flops 896 | bytes 7168 | tf_op jit(solution)/shard_map/pmax | solution.py:44
  233.3 2.7 fusion.2
  236.1 30.1 %gather_fusion = f32[896]{0:T(1024)S(1)} fusion(f32[896,1000]{0,1:T(8,128)} %get-tuple-element.17, s32[896]{0:T(1024)S(1)} %fusion.6), kind=kCustom, calls=%fused_computation | custom fusion | bytes 14336 | tf_op jit(solution)/shard_map/jit(take_along_axis)/gather | solution.py:39
  266.3 125.6 %all-reduce.1 = (f32[896]{0:T(1024)S(1)}, f32[896]{0:T(1024)S(1)}, f32[896]{0:T(1024)S(1)}) all-reduce(f32[896]{0:T(1024)S(1)} %select_select_fusion, f32[896]{0:T(1024)S(1)} %get-tuple-element.13, f32[896]{0:T(1024)S(1)} %get-tuple-element.12), channel_id=1, replica_groups=mesh['dp'=16,'tensor'=32] {'tensor'}, use_global_device_ids=true, to_apply=%region_1.0 | all-reduce | flops 2688 | bytes 21504 | tf_op jit(solution)/shard_map/psum | solution.py:46
  391.9 0.6 subtract_multiply_fusion
  392.4 0.0 copy-start.1
  392.5 0.0 copy-done.3
  392.5 0.1 select_reduce_fusion
  392.6 107.4 %all-reduce = (f32[64]{0:T(128)S(1)}, f32[64]{0:T(128)S(1)}) all-reduce(f32[64]{0:T(128)S(1)} %get-tuple-element.6, f32[64]{0:T(128)S(1)} %get-tuple-element.5), channel_id=1, replica_groups=mesh['dp'=16,'tensor'=32] {'dp','tensor'}, use_global_device_ids=true, to_apply=%region_9.10 | all-reduce | flops 128 | bytes 1024 | tf_op jit(solution)/shard_map/psum | solution.py:61
  500.0 0.5 maximum_divide_fusion
  500.5 0.0 copy-done.1
  (10 shorter events, 0.1 us)
Async XLA Ops:
  7.2 149.5 %all-gather.3.cloned.1.call-start = ((), (), s32[]{:S(2)}) async-start(), calls=%async_computation.1 | async-start | bytes 8704000 | tf_op jit(solution)/shard_map/all_gather | solution.py:29
  13.0 11.5 %copy-start.2 = (bf16[128]{0:T(256)(128)(2,1)S(1)}, bf16[128]{0:T(256)(128)(2,1)}, u32[]{:S(2)}) copy-start(bf16[128]{0:T(256)(128)(2,1)} %param.7) | copy-start | bytes 772
  13.1 130.9 %copy-start = (s32[896]{0:T(1024)S(1)}, s32[896]{0:T(1024)}, u32[]{:S(2)}) copy-start(s32[896]{0:T(1024)} %param.9) | copy-start | bytes 10756
  13.1 131.0 %copy-start.4 = (s32[28]{0:T(128)S(1)}, s32[28]{0:T(128)}, u32[]{:S(2)}) copy-start(s32[28]{0:T(128)} %param.11) | copy-start | bytes 340
  13.1 131.0 %all-to-all-start = ((bf16[32,896,128]{1,2,0:T(8,128)(2,1)}), bf16[32,896,128]{1,2,0:T(8,128)(2,1)}, u32[]{:S(2)}, u32[]{:S(2)}) async-start(bf16[32,896,128]{1,2,0:T(8,128)(2,1)} %stack.2), calls=%async_computation | async-start | bytes 14680064 | tf_op jit(solution)/shard_map/all_to_all | solution.py:11
  171.2 221.3 %copy-start.3 = (s32[28]{0:T(128)S(1)}, s32[28]{0:T(128)}, u32[]{:S(2)}) copy-start(s32[28]{0:T(128)} %param.10) | copy-start | bytes 340
  392.4 108.1 %copy-start.1 = (f32[28]{0:T(128)}, f32[28]{0:T(128)S(1)}, u32[]{:S(2)}) copy-start(f32[28]{0:T(128)S(1)} %get-tuple-element.15) | copy-start | bytes 340
Sparse Core Ops, SparseCore 0:
  10.0 121.7 all-gather.2
